TPU v7x, 32 devices: a whole 2x2x4 slice. The times are simulated.
32 devices in a mesh: rows: 4 (over x, core), cols: 8 (over z, y).
Axes of the slice: x: 2, y: 2, z: 4, core: 2. Of those that a mesh axis runs over, the one named last changes fastest.
Arguments:
- pair_integrals: float32 [4096, 4096], P('rows', 'cols'), may hold values from -6 to 6
- left_factor: float32 [4096, 1024], P('rows', 'cols'), may hold values from -0.9375 to 0.9375
- core: float32 [1024, 1024], replicated, may hold values from -6 to 6
- right_factor: float32 [4096, 1024], P('cols', 'rows'), may hold values from -0.9375 to 0.9375
Outputs:
- core_next: float32 [1024, 1024], replicated
All inputs are finite; a program needn't handle non-finite values.
Results may differ from a plain program's by a relative error of at most 0.000062.
Values sent between devices are 32-bit elements; how exact they have to be, the bound alone decides.
No kernel may reach another device: no remote copies, remote signals or barrier semaphores. Data moves between devices by JAX's collectives and lax.ppermute only.
A program may use at most 128 MiB of HBM per device.

v0:
```python
import jax
import jax.numpy as jnp
from jax import lax
from jax.sharding import PartitionSpec as P


def product(left, right):
    return jnp.dot(left, right, precision=lax.Precision.HIGHEST, preferred_element_type=jnp.float32)


def shards(pair_integrals, left_factor, core, right_factor):
    left_rows = lax.all_gather(left_factor, "cols", axis=1, tiled=True)
    right_rows = lax.all_gather(right_factor, "rows", axis=1, tiled=True)
    mixed = product(core, right_rows.T)
    residual = pair_integrals - product(left_rows, mixed)
    along = product(residual, right_rows)
    local_term = product(left_rows.T, along)
    gradient = lax.psum(local_term, ("rows", "cols"))
    numer = jnp.sum(gradient * gradient)
    image = product(left_rows, product(gradient, right_rows.T))
    denom = lax.psum(jnp.sum(image * image), ("rows", "cols"))
    return core + numer / denom * gradient


def solution(mesh):
    return jax.shard_map(
        shards,
        mesh=mesh,
        in_specs=(P("rows", "cols"), P("rows", "cols"), P(), P("cols", "rows")),
        out_specs=P(),
        check_vma=False,
    )
```

profile of v0, /device:TPU:0, one launch (start us, length us, event | category | flops | bytes accessed | tf_op | source)
XLA Modules:
  0.0 382.8 jit_solution(6131846957028007544)
XLA Ops:
  6.5 0.0 all-gather.3.cloned.1.call-start
  6.5 0.7 all-gather.3.cloned.1.call-update
  7.3 0.0 all-gather.5.cloned.1.call-start
  7.3 0.7 all-gather.5.cloned.1.call-update
  8.0 0.0 all-reduce.2.cloned.1.call-start
  8.1 26.2 %all-gather.3.cloned.1.call-done = f32[512,1024]{1,0:T(8,128)} async-done(((f32[512,256]{1,0:T(8,128)}), f32[512,1024]{1,0:T(8,128)}) %all-gather.3.cloned.1.call-update) | async-done | bytes 2097168 | tf_op jit(solution)/shard_map/all_gather | solution.py:13
  34.2 10.2 %fusion.1 = f32[1024,512]{1,0:T(8,128)} fusion(f32[1024,1024]{1,0:T(8,128)} %param.6, f32[512,1024]{1,0:T(8,128)} %all-gather.3.cloned.1.call-done), kind=kOutput, calls=%fused_computation.6 | convolution fusion | flops 6442450944 | bytes 8388608 | tf_op jit(solution)/shard_map/dot_general | solution.py:8
  44.5 0.0 copy-start
  44.5 66.5 %all-gather.5.cloned.1.call-done = f32[1024,1024]{1,0:T(8,128)} async-done(((f32[1024,128]{1,0:T(8,128)}), f32[1024,1024]{1,0:T(8,128)}) %all-gather.5.cloned.1.call-update) | async-done | bytes 4194320 | tf_op jit(solution)/shard_map/all_gather | solution.py:12
  110.9 0.0 copy-start.3
  110.9 10.0 %fusion.2 = f32[512,1024]{0,1:T(8,128)S(1)} fusion(f32[1024,512]{1,0:T(8,128)} %fusion.1, f32[1024,1024]{1,0:T(8,128)} %all-gather.5.cloned.1.call-done), kind=kOutput, calls=%fused_computation.7 | convolution fusion | flops 6442450944 | bytes 8388608 | tf_op jit(solution)/shard_map/dot_general | solution.py:8
  120.9 0.0 copy-done
  120.9 0.0 copy-done.3
  120.9 0.0 copy-start.1
  120.9 6.9 %fusion = f32[1024,1024]{1,0:T(8,128)S(1)} fusion(f32[512,1024]{1,0:T(8,128)S(1)} %copy-done, f32[1024,512]{1,0:T(8,128)S(1)} %copy-done.3, f32[512,1024]{0,1:T(8,128)S(1)} %fusion.2), kind=kOutput, calls=%fused_computation.4 | convolution fusion | flops 6442975232 | bytes 10485760 | tf_op jit(solution)/shard_map/dot_general | solution.py:8
  127.8 0.0 copy-done.1
  127.8 14.9 %convolution_bitcast_fusion = f32[1024,1024]{0,1:T(8,128)} fusion(f32[1024,1024]{1,0:T(8,128)S(1)} %fusion, f32[1024,1024]{1,0:T(8,128)S(1)} %copy-done.1), kind=kOutput, calls=%fused_computation.2 | convolution fusion | flops 12884901888 | bytes 12582912 | tf_op jit(solution)/shard_map/dot_general | solution.py:8
  142.7 0.0 all-reduce.2.cloned.1.call-update
  142.7 140.8 %all-reduce.2.cloned.1.call-done = f32[1024,1024]{0,1:T(8,128)} async-done(((f32[1024,1024]{0,1:T(8,128)}), f32[1024,1024]{0,1:T(8,128)}) %all-reduce.2.cloned.1.call-update) | async-done | bytes 4194320 | tf_op jit(solution)/shard_map/psum | solution.py:18
  283.5 0.0 copy-start.2
  283.5 15.6 %fusion.3 = f32[1024,512]{1,0:T(8,128)S(1)} fusion(f32[1024,1024]{0,1:T(8,128)} %all-reduce.2.cloned.1.call-done, f32[512,1024]{1,0:T(8,128)S(1)} %copy-done), kind=kOutput, calls=%fused_computation.8 | convolution fusion | flops 6442450944 | bytes 8388608 | tf_op jit(solution)/shard_map/dot_general | solution.py:8
  299.2 0.0 copy-done.2
  299.2 14.3 %multiply_reduce_fusion.1 = f32[]{:T(128)} fusion(f32[1024,512]{1,0:T(8,128)S(1)} %fusion.3, f32[1024,1024]{1,0:T(8,128)S(1)} %copy-done.2), kind=kOutput, calls=%fused_computation.5 | convolution fusion | flops 6443499520 | bytes 6291460 | tf_op jit(solution)/shard_map/dot_general | solution.py:8
  313.5 5.3 %copy.5 = f32[1024,1024]{0,1:T(8,128)} copy(f32[1024,1024]{1,0:T(8,128)} %param.6) | data formatting | bytes 8388608 | tf_op args[2]
  318.9 39.5 %psum.15 = f32[]{:T(128)} all-reduce(f32[]{:T(128)} %multiply_reduce_fusion.1), channel_id=1, replica_groups=mesh['rows'=4,'cols'=8] {'rows','cols'}, use_global_device_ids=true, to_apply=%region_3.0 | all-reduce | flops 1 | bytes 8 | tf_op jit(solution)/shard_map/psum | solution.py:21
  358.3 3.9 %multiply_reduce_fusion = f32[]{:T(128)} fusion(f32[1024,1024]{0,1:T(8,128)} %all-reduce.2.cloned.1.call-done), kind=kLoop, calls=%fused_computation.1 | loop fusion | flops 2097151 | bytes 4194308 | tf_op jit(solution)/shard_map/reduce_sum | solution.py:19
  363.6 6.9 %multiply_add_fusion = f32[1024,1024]{0,1:T(8,128)} fusion(f32[1024,1024]{0,1:T(8,128)} %copy.5, f32[1024,1024]{0,1:T(8,128)} %all-reduce.2.cloned.1.call-done, f32[]{:T(128)S(6)} %div.3), kind=kLoop, calls=%fused_computation | loop fusion | flops 2097152 | bytes 12582916 | tf_op jit(solution)/shard_map/add | solution.py:22
  370.4 5.3 %copy.6 = f32[1024,1024]{1,0:T(8,128)} copy(f32[1024,1024]{0,1:T(8,128)} %multiply_add_fusion) | data formatting | bytes 8388608 | tf_op jit(solution)/shard_map/add | solution.py:22
Async XLA Ops:
  6.5 27.7 %all-gather.3.cloned.1.call-start = ((), (), s32[]{:S(2)}) async-start(), calls=%async_computation | async-start | bytes 2621440 | tf_op jit(solution)/shard_map/all_gather | solution.py:13
  7.3 103.7 %all-gather.5.cloned.1.call-start = ((), (), s32[]{:S(2)}) async-start(), calls=%async_computation.1 | async-start | bytes 4718592 | tf_op jit(solution)/shard_map/all_gather | solution.py:12
  8.0 275.5 %all-reduce.2.cloned.1.call-start = ((), (), s32[]{:S(2)}) async-start(), calls=%async_computation.2 | async-start | bytes 8388608 | tf_op jit(solution)/shard_map/psum | solution.py:18
  44.5 76.4 %copy-start = (f32[512,1024]{1,0:T(8,128)S(1)}, f32[512,1024]{1,0:T(8,128)}, u32[]{:S(2)}) copy-start(f32[512,1024]{1,0:T(8,128)} %all-gather.3.cloned.1.call-done) | copy-start | bytes 6291460
  110.9 10.0 %copy-start.3 = (f32[1024,512]{1,0:T(8,128)S(1)}, f32[1024,512]{1,0:T(8,128)}, u32[]{:S(2)}) copy-start(f32[1024,512]{1,0:T(8,128)} %param.4) | copy-start | bytes 6291460
  120.9 6.9 %copy-start.1 = (f32[1024,1024]{1,0:T(8,128)S(1)}, f32[1024,1024]{1,0:T(8,128)}, u32[]{:S(2)}) copy-start(f32[1024,1024]{1,0:T(8,128)} %all-gather.5.cloned.1.call-done) | copy-start | bytes 12582916
  283.5 15.6 %copy-start.2 = (f32[1024,1024]{1,0:T(8,128)S(1)}, f32[1024,1024]{1,0:T(8,128)}, u32[]{:S(2)}) copy-start(f32[1024,1024]{1,0:T(8,128)} %all-gather.5.cloned.1.call-done) | copy-start | bytes 12582916
Sparse Core Ops, SparseCore 0:
  8.9 25.2 all-gather.2
  36.2 74.6 all-gather.4
  142.9 140.6 all-reduce.1
where the time goes:
time: 389 us; the launch traced here: 383 us
  waiting for transfers between devices  235 us (60%)
  matrix products  72 us (19%)
  blocking collectives  39.5 us (10%)
  between operations  15 us (4%)
  other arithmetic  10.8 us (3%)
  local copies, waits for them, and re-layouts  10.7 us (3%)
    psum x1, waiting for transfers between devices, shards(): gradient = lax.psum(local_term, ('rows', 'cols'))  141 us
    dot_general x6, matrix products, product(): jnp.dot(left, right, precision=lax.Precision.HIGHEST, preferred_element_t...  72 us
    all_gather x1, waiting for transfers between devices, shards(): left_rows = lax.all_gather(left_factor, 'cols', axis=1, tiled=True)  66.5 us
    psum x1, blocking collectives, shards(): denom = lax.psum(jnp.sum(image * image), ('rows', 'cols'))  39.5 us
    all_gather x1, waiting for transfers between devices, shards(): right_rows = lax.all_gather(right_factor, 'rows', axis=1, tiled=True)  26.2 us
  transfers between devices with their start and end apart: 3, of which 3 were waited for; matrix products, arithmetic and copies ran while one was open for 3% of the time, Pallas kernels for 0%

commit v1 on v0

--- a/solution.py
+++ b/solution.py
@@ -1,7 +1,18 @@
+import functools
 import jax
 import jax.numpy as jnp
 from jax import lax
 from jax.sharding import PartitionSpec as P
+from jax.lax import psum
+
+
+def track_the_words(mine, group_axis, ax_name):
+    for hop_no in (group_axis, ax_name):
+        mine = psum(mine, hop_no)
+    return mine
+
+
+close_the_corner = functools.partial(track_the_words, group_axis="cols", ax_name="rows")
 
 
 def product(left, right):
@@ -15,7 +26,7 @@
     residual = pair_integrals - product(left_rows, mixed)
     along = product(residual, right_rows)
     local_term = product(left_rows.T, along)
-    gradient = lax.psum(local_term, ("rows", "cols"))
+    gradient = close_the_corner(local_term)
     numer = jnp.sum(gradient * gradient)
     image = product(left_rows, product(gradient, right_rows.T))
     denom = lax.psum(jnp.sum(image * image), ("rows", "cols"))

time: 389 us -> 490 us (1.26)
  waiting for transfers between devices: 235 us -> 335 us
    psum x1 -> x2, waiting for transfers between devices: 141 us -> 241 us  [track_the_words(): mine = psum(mine, hop_no)]
  transfers between devices with their start and end apart: 3 -> 4, of which waited for: 3 -> 4; matrix products, arithmetic and copies ran while one was open for 3% -> 2% of each run, Pallas kernels for 0% -> 0%
where the time goes in v1:
time: 490 us; the launch traced here: 484 us
  waiting for transfers between devices  335 us (68%)
  matrix products  72 us (15%)
  blocking collectives  39.6 us (8%)
  between operations  15 us (3%)
  other arithmetic  10.8 us (2%)
  local copies, waits for them, and re-layouts  10.7 us (2%)
    psum x2, waiting for transfers between devices, track_the_words(): mine = psum(mine, hop_no)  241 us
    dot_general x6, matrix products, product(): jnp.dot(left, right, precision=lax.Precision.HIGHEST, preferred_element_t...  72 us
    all_gather x1, waiting for transfers between devices, shards(): left_rows = lax.all_gather(left_factor, 'cols', axis=1, tiled=True)  66.5 us
    psum x1, blocking collectives, shards(): denom = lax.psum(jnp.sum(image * image), ('rows', 'cols'))  39.6 us
    all_gather x1, waiting for transfers between devices, shards(): right_rows = lax.all_gather(right_factor, 'rows', axis=1, tiled=True)  26.2 us
  transfers between devices with their start and end apart: 4, of which 4 were waited for; matrix products, arithmetic and copies ran while one was open for 2% of the time, Pallas kernels for 0%

profile of v1, /device:TPU:0, one launch (start us, length us, event | category | flops | bytes accessed | tf_op | source)
XLA Modules:
  0.0 483.5 jit_solution(4981012401085414892)
XLA Ops:
  6.5 0.0 all-gather.3.cloned.1.call-start
  6.5 0.7 all-gather.3.cloned.1.call-update
  7.3 0.0 all-gather.5.cloned.1.call-start
  7.3 0.7 all-gather.5.cloned.1.call-update
  8.0 0.0 all-reduce.3.cloned.1.call-start
  8.1 26.2 %all-gather.3.cloned.1.call-done = f32[512,1024]{1,0:T(8,128)} async-done(((f32[512,256]{1,0:T(8,128)}), f32[512,1024]{1,0:T(8,128)}) %all-gather.3.cloned.1.call-update) | async-done | bytes 2097168 | tf_op jit(solution)/shard_map/all_gather | solution.py:24
  34.2 10.2 %fusion.1 = f32[1024,512]{1,0:T(8,128)} fusion(f32[1024,1024]{1,0:T(8,128)} %param.6, f32[512,1024]{1,0:T(8,128)} %all-gather.3.cloned.1.call-done), kind=kOutput, calls=%fused_computation.6 | convolution fusion | flops 6442450944 | bytes 8388608 | tf_op jit(solution)/shard_map/dot_general | solution.py:19
  44.5 0.0 copy-start
  44.5 66.5 %all-gather.5.cloned.1.call-done = f32[1024,1024]{1,0:T(8,128)} async-done(((f32[1024,128]{1,0:T(8,128)}), f32[1024,1024]{1,0:T(8,128)}) %all-gather.5.cloned.1.call-update) | async-done | bytes 4194320 | tf_op jit(solution)/shard_map/all_gather | solution.py:23
  110.9 0.0 copy-start.3
  110.9 10.0 %fusion.2 = f32[512,1024]{0,1:T(8,128)S(1)} fusion(f32[1024,512]{1,0:T(8,128)} %fusion.1, f32[1024,1024]{1,0:T(8,128)} %all-gather.5.cloned.1.call-done), kind=kOutput, calls=%fused_computation.7 | convolution fusion | flops 6442450944 | bytes 8388608 | tf_op jit(solution)/shard_map/dot_general | solution.py:19
  120.9 0.0 copy-done
  120.9 0.0 copy-done.3
  120.9 0.0 copy-start.1
  120.9 6.9 %fusion = f32[1024,1024]{1,0:T(8,128)S(1)} fusion(f32[512,1024]{1,0:T(8,128)S(1)} %copy-done, f32[1024,512]{1,0:T(8,128)S(1)} %copy-done.3, f32[512,1024]{0,1:T(8,128)S(1)} %fusion.2), kind=kOutput, calls=%fused_computation.4 | convolution fusion | flops 6442975232 | bytes 10485760 | tf_op jit(solution)/shard_map/dot_general | solution.py:19
  127.8 0.0 copy-done.1
  127.8 14.9 %convolution_bitcast_fusion = f32[1024,1024]{0,1:T(8,128)} fusion(f32[1024,1024]{1,0:T(8,128)S(1)} %fusion, f32[1024,1024]{1,0:T(8,128)S(1)} %copy-done.1), kind=kOutput, calls=%fused_computation.2 | convolution fusion | flops 12884901888 | bytes 12582912 | tf_op jit(solution)/shard_map/dot_general | solution.py:19
  142.7 0.0 all-reduce.3.cloned.1.call-update
  142.7 0.0 all-reduce.5.cloned.1.call-start
  142.8 154.6 %all-reduce.3.cloned.1.call-done = f32[1024,1024]{0,1:T(8,128)} async-done(((f32[1024,1024]{0,1:T(8,128)}), f32[1024,1024]{0,1:T(8,128)}) %all-reduce.3.cloned.1.call-update) | async-done | bytes 4194320 | tf_op jit(solution)/shard_map/psum | solution.py:11
  297.4 0.0 all-reduce.5.cloned.1.call-update
  297.5 86.7 %all-reduce.5.cloned.1.call-done = f32[1024,1024]{0,1:T(8,128)} async-done(((f32[1024,1024]{0,1:T(8,128)}), f32[1024,1024]{0,1:T(8,128)}) %all-reduce.5.cloned.1.call-update) | async-done | bytes 4194320 | tf_op jit(solution)/shard_map/psum | solution.py:11
  384.2 0.0 copy-start.2
  384.2 15.6 %fusion.3 = f32[1024,512]{1,0:T(8,128)S(1)} fusion(f32[1024,1024]{0,1:T(8,128)} %all-reduce.5.cloned.1.call-done, f32[512,1024]{1,0:T(8,128)S(1)} %copy-done), kind=kOutput, calls=%fused_computation.8 | convolution fusion | flops 6442450944 | bytes 8388608 | tf_op jit(solution)/shard_map/dot_general | solution.py:19
  399.8 0.0 copy-done.2
  399.8 14.3 %multiply_reduce_fusion.1 = f32[]{:T(128)} fusion(f32[1024,512]{1,0:T(8,128)S(1)} %fusion.3, f32[1024,1024]{1,0:T(8,128)S(1)} %copy-done.2), kind=kOutput, calls=%fused_computation.5 | convolution fusion | flops 6443499520 | bytes 6291460 | tf_op jit(solution)/shard_map/dot_general | solution.py:19
  414.1 5.3 %copy.5 = f32[1024,1024]{0,1:T(8,128)} copy(f32[1024,1024]{1,0:T(8,128)} %param.6) | data formatting | bytes 8388608 | tf_op args[2]
  419.5 39.6 %psum.23 = f32[]{:T(128)} all-reduce(f32[]{:T(128)} %multiply_reduce_fusion.1), channel_id=1, replica_groups=mesh['rows'=4,'cols'=8] {'rows','cols'}, use_global_device_ids=true, to_apply=%region_4.0 | all-reduce | flops 1 | bytes 8 | tf_op jit(solution)/shard_map/psum | solution.py:32
  459.0 3.9 multiply_reduce_fusion
  464.3 6.9 %multiply_add_fusion = f32[1024,1024]{0,1:T(8,128)} fusion(f32[1024,1024]{0,1:T(8,128)} %copy.5, f32[1024,1024]{0,1:T(8,128)} %all-reduce.5.cloned.1.call-done, f32[]{:T(128)S(6)} %div.3), kind=kLoop, calls=%fused_computation | loop fusion | flops 2097152 | bytes 12582916 | tf_op jit(solution)/shard_map/add | solution.py:33
  471.2 5.3 %copy.6 = f32[1024,1024]{1,0:T(8,128)} copy(f32[1024,1024]{0,1:T(8,128)} %multiply_add_fusion) | data formatting | bytes 8388608 | tf_op jit(solution)/shard_map/add | solution.py:33
Async XLA Ops:
  6.5 27.7 %all-gather.3.cloned.1.call-start = ((), (), s32[]{:S(2)}) async-start(), calls=%async_computation | async-start | bytes 2621440 | tf_op jit(solution)/shard_map/all_gather | solution.py:24
  7.3 103.7 %all-gather.5.cloned.1.call-start = ((), (), s32[]{:S(2)}) async-start(), calls=%async_computation.1 | async-start | bytes 4718592 | tf_op jit(solution)/shard_map/all_gather | solution.py:23
  8.0 289.4 %all-reduce.3.cloned.1.call-start = ((), (), s32[]{:S(2)}) async-start(), calls=%async_computation.2 | async-start | bytes 8388608 | tf_op jit(solution)/shard_map/psum | solution.py:11
  44.5 76.4 %copy-start = (f32[512,1024]{1,0:T(8,128)S(1)}, f32[512,1024]{1,0:T(8,128)}, u32[]{:S(2)}) copy-start(f32[512,1024]{1,0:T(8,128)} %all-gather.3.cloned.1.call-done) | copy-start | bytes 6291460
  110.9 10.0 %copy-start.3 = (f32[1024,512]{1,0:T(8,128)S(1)}, f32[1024,512]{1,0:T(8,128)}, u32[]{:S(2)}) copy-start(f32[1024,512]{1,0:T(8,128)} %param.4) | copy-start | bytes 6291460
  120.9 6.9 %copy-start.1 = (f32[1024,1024]{1,0:T(8,128)S(1)}, f32[1024,1024]{1,0:T(8,128)}, u32[]{:S(2)}) copy-start(f32[1024,1024]{1,0:T(8,128)} %all-gather.5.cloned.1.call-done) | copy-start | bytes 12582916
  142.7 241.4 %all-reduce.5.cloned.1.call-start = ((), (), s32[]{:S(2)}) async-start(), calls=%async_computation.3 | async-start | bytes 8388608 | tf_op jit(solution)/shard_map/psum | solution.py:11
  384.2 15.6 %copy-start.2 = (f32[1024,1024]{1,0:T(8,128)S(1)}, f32[1024,1024]{1,0:T(8,128)}, u32[]{:S(2)}) copy-start(f32[1024,1024]{1,0:T(8,128)} %all-gather.5.cloned.1.call-done) | copy-start | bytes 12582916
Sparse Core Ops, SparseCore 0:
  8.9 25.2 all-gather.2
  36.2 74.6 all-gather.4
  142.9 154.5 all-reduce.2
  299.7 84.4 all-reduce.4
